TPU v7x, 32 devices: a whole 2x2x4 slice. The times are simulated.
32 devices in a mesh: ra: 4 (over z), dec: 8 (over y, x, core).
Axes of the slice: x: 2, y: 2, z: 4, core: 2. Of those that a mesh axis runs over, the one named last changes fastest.
Arguments:
- forests: bfloat16 [8, 32, 128, 1024], P('ra', 'dec'), may hold values from -6 to 6
- resolution: float32 [8, 32, 128], P('ra', 'dec'), may hold values from 0.3 to 1.2
- pixel_range: int32 [8, 32, 2, 128], P('ra', 'dec'), may hold values from 0 to 1024, as said below
- block_pairs: int32 [4, 8, 40, 3], P('ra', 'dec'), may hold values from -1 to 7, as said below
- block_count: int32 [4, 8], P('ra', 'dec'), may hold values from 10 to 40, as said below
- separation_bin: int32 [4, 8, 40, 128, 128], P('ra', 'dec'), may hold values from 0 to 8
Outputs:
- tile_power: float32 [4, 8, 8, 128], P('ra', 'dec')
- sky_power: float32 [8, 128], replicated
Inputs may be any that keep to these rules, and one draw needn't show every extreme that they name: `pixel_range`: lo < hi for every forest; at least 256 valid pixels. `block_pairs`: each device's list names every one of its own cells once with each of the five offsets (0, 0), (0, 1), (1, -1), (1, 0), (1, 1), in an order drawn from the seed. Slots at or past block_count are ignored. `block_count`: some device has all 40 slots live in every draw.
All inputs are finite; a program needn't handle non-finite values.
Results may differ from a plain program's by a relative error of at most 0.0037.
Values may be sent and summed in bfloat16 or wider, within the bound.
No kernel may reach another device: no remote copies, remote signals or barrier semaphores. Data moves between devices by JAX's collectives and lax.ppermute only.
A program may use at most 64 MiB of HBM per device.

v0:
```python
import jax
import jax.numpy as jnp
from jax import lax
from jax.sharding import PartitionSpec as P

NSEP = 8
NKB = 128


def extended(block, sides, width):
    for axis, dim in sides:
        count = lax.axis_size(axis)
        forward = [(i, i + 1) for i in range(count - 1)]
        backward = [(target, source) for source, target in forward]
        low = lax.ppermute(
            lax.slice_in_dim(block, block.shape[dim] - width, None, axis=dim), axis, forward
        )
        high = lax.ppermute(lax.slice_in_dim(block, 0, width, axis=dim), axis, backward)
        block = jnp.concatenate([low, block, high], axis=dim)
    return block


def from_behind(value, axis, steps):
    count = lax.axis_size(axis)
    leading, last = (max(0, -steps), min(count, count - steps))
    return lax.ppermute(value, axis, [(source, source + steps) for source in range(leading, last)])


def dft_table(length, n_modes):
    sample = jnp.arange(length, dtype=jnp.int32)[:, None]
    mode_index = jnp.arange(n_modes, dtype=jnp.int32)[None, :]
    angles = (sample * mode_index % length).astype(jnp.float32) * (2.0 * jnp.pi / length)
    return jnp.concatenate([jnp.cos(angles), jnp.sin(angles)], axis=1).astype(jnp.bfloat16)


def kbin_table(n_modes, n_bins):
    column = jnp.arange(2 * n_modes, dtype=jnp.int32) % n_modes
    which = column // (n_modes // n_bins)
    return (which[:, None] == jnp.arange(n_bins, dtype=jnp.int32)[None, :]).astype(jnp.float32)


def mask_pixels(flux, pixel_range):
    position = jnp.arange(flux.shape[-1], dtype=jnp.int32)
    lower = pixel_range[..., 0, :][..., None]
    upper = pixel_range[..., 1, :][..., None]
    inside = (position >= lower) & (position < upper)
    return jnp.where(inside, flux, jnp.zeros_like(flux))


def to_spectra(masked, widths, basis):
    length = basis.shape[0]
    n_modes = basis.shape[1] // 2
    raw = jnp.dot(masked, basis, preferred_element_type=jnp.float32)
    wavenum = jnp.arange(n_modes, dtype=jnp.float32) * (2.0 * jnp.pi / length)
    wavenum = jnp.concatenate([wavenum, wavenum])
    window = jnp.exp(-0.5 * (wavenum * widths[..., None]) ** 2)
    return (raw * window).astype(jnp.bfloat16)


def block_term(grid_flat, index_a, index_b, sep_bins):
    n_sep = NSEP
    per_cell = sep_bins.shape[0]
    left = lax.dynamic_index_in_dim(grid_flat, index_a, 0, keepdims=False)
    right = lax.dynamic_index_in_dim(grid_flat, index_b, 0, keepdims=False)
    onehot = (sep_bins[None, :, :] == jnp.arange(n_sep, dtype=jnp.int32)[:, None, None]).astype(
        jnp.bfloat16
    )
    mixed = jnp.dot(
        onehot.reshape(n_sep * per_cell, per_cell), right, preferred_element_type=jnp.float32
    )
    mixed = mixed.reshape(n_sep, per_cell, -1)
    block_sum = jnp.sum(mixed * left.astype(jnp.float32)[None], axis=1)
    pair_counts = jnp.sum(onehot.reshape(n_sep, -1).astype(jnp.float32), axis=1)
    return (block_sum, pair_counts)


def per_device(forests, resolution, pixel_range, block_pairs, block_count, separation_bin):
    cells_ra, cells_dec, per_cell, length = forests.shape
    basis = dft_table(length, length // 2)
    masked = mask_pixels(forests, pixel_range)
    own_spectra = to_spectra(masked, resolution, basis)
    sided = extended(own_spectra, (("dec", 1),), 1)
    above = from_behind(sided[0:1], "ra", -1)
    padded = jnp.concatenate([sided, above], axis=0)
    cols_pad = cells_dec + 2
    grid_flat = padded.reshape(-1, per_cell, length)
    entries = block_pairs[0, 0]
    sep_bins = separation_bin[0, 0]
    live_count = block_count[0, 0]

    def slot_term(slot_index):
        entry_row = entries[slot_index]
        row_a = entry_row[0] // cells_dec
        col_a = entry_row[0] % cells_dec + 1
        index_a = row_a * cols_pad + col_a
        index_b = (row_a + entry_row[1]) * cols_pad + col_a + entry_row[2]
        return block_term(grid_flat, index_a, index_b, sep_bins[slot_index])

    start_value = (jnp.zeros((NSEP, length), jnp.float32), jnp.zeros((NSEP,), jnp.float32))

    def add_live(slot_index, carry):
        block_sum, counts = slot_term(slot_index)
        return (carry[0] + block_sum, carry[1] + counts)

    sums, counts = lax.fori_loop(0, live_count, add_live, start_value)
    binned = jnp.dot(sums, kbin_table(length // 2, NKB), precision=lax.Precision.HIGHEST)
    tile_power = (binned / (per_cell * length)).reshape(1, 1, NSEP, NKB)
    summed, all_counts = lax.psum((binned, counts), ("ra", "dec"))
    sky_power = summed / jnp.maximum(all_counts, 1.0)[:, None]
    return (tile_power, sky_power)


def solution(mesh):
    in_specs = (
        P("ra", "dec", None, None),
        P("ra", "dec", None),
        P("ra", "dec", None, None),
        P("ra", "dec", None, None),
        P("ra", "dec"),
        P("ra", "dec", None, None, None),
    )
    out_specs = (P("ra", "dec", None, None), P())
    return jax.shard_map(
        per_device, mesh=mesh, in_specs=in_specs, out_specs=out_specs, check_vma=False
    )
```

profile of v0, /device:TPU:0, one launch (start us, length us, event | category | flops | bytes accessed | tf_op | source)
XLA Modules:
  0.0 456.6 jit_solution(12260927048021557537)
XLA Ops:
  0.7 8.5 %sine_convert_fusion = (bf16[1024,512]{1,0:T(8,128)(2,1)S(1)}, bf16[1024,512]{1,0:T(8,128)(2,1)S(1)}) fusion(), kind=kLoop, calls=%fused_computation.29 | loop fusion | flops 8388608 | bytes 2097152 | tf_op jit(solution)/shard_map/convert.2
  9.2 2.9 multiply_convert_fusion
  12.2 2.4 collective-permute-start
  16.1 4.4 collective-permute-done.1
  23.2 28.7 %collective-permute-done.2 = bf16[1,6,128,1024]{3,2,1,0:T(8,128)(2,1)} collective-permute-done((bf16[1,6,128,1024]{3,2,1,0:T(8,128)(2,1)}, bf16[1,6,128,1024]{3,2,1,0:T(8,128)(2,1)}, u32[]{:S(2)}, u32[]{:S(2)}) %collective-permute-start.2) | collective-permute-done | bytes 1572896 | tf_op jit(solution)/shard_map/ppermute | solution.py:26
  51.8 3.6 pad_maximum_fusion
  55.4 343.0 %while.14 = (s32[]{:T(128)}, f32[8,1024]{1,0:T(8,128)S(1)}, f32[8]{0:T(128)S(1)}, s32[]{:T(128)}, s32[40,128,128]{2,1,0:T(8,128)}, /*index=5*/s32[40,3]{0,1:T(4,...) while((s32[]{:T(128)}, f32[8,1024]{1,0:T(8,128)S(1)}, ...), condition=%wide.region_3.4_spmd, body=%wide.region_0.3_spmd.sunk | while | flops 271319072 | bytes 2032330 | solution.py:105
  80.5 1.7 multiply_reduce_fusion.2
  89.5 1.7 multiply_reduce_fusion.2
  98.5 1.7 multiply_reduce_fusion.2
  107.5 1.7 multiply_reduce_fusion.2
  143.5 1.7 multiply_reduce_fusion.2
  161.5 1.7 multiply_reduce_fusion.2
  170.6 1.7 multiply_reduce_fusion.2
  179.6 1.7 multiply_reduce_fusion.2
  188.6 1.7 multiply_reduce_fusion.2
  215.6 1.7 multiply_reduce_fusion.2
  224.6 1.7 multiply_reduce_fusion.2
  233.6 1.7 multiply_reduce_fusion.2
  242.6 1.7 multiply_reduce_fusion.2
  251.6 1.7 multiply_reduce_fusion.2
  287.7 1.7 multiply_reduce_fusion.2
  305.7 1.7 multiply_reduce_fusion.2
  314.7 1.7 multiply_reduce_fusion.2
  323.7 1.7 multiply_reduce_fusion.2
  332.7 1.7 multiply_reduce_fusion.2
  359.8 1.7 multiply_reduce_fusion.2
  368.8 1.7 multiply_reduce_fusion.2
  377.8 1.7 multiply_reduce_fusion.2
  386.8 1.7 multiply_reduce_fusion.2
  395.8 1.7 multiply_reduce_fusion.2
  399.4 56.5 %all-reduce = (f32[8,128]{1,0:T(8,128)S(1)}, f32[8]{0:T(128)S(1)}) all-reduce(f32[8,128]{1,0:T(8,128)S(1)} %fusion.21, f32[8]{0:T(128)S(1)} %get-tuple-element.99), channel_id=1, replica_groups=mesh['ra'=4,'dec'=8] {'ra','dec'}, use_global_device_ids=true, to_apply=%region_4.5 | all-reduce | flops 1032 | bytes 8256 | tf_op jit(solution)/shard_map/psum | solution.py:108
  (304 shorter events, 134.9 us)
Async XLA Ops:
  0.6 8.5 %copy-start = (s32[2,4,2,128]{3,2,1,0:T(2,128)S(1)}, s32[2,4,2,128]{3,2,1,0:T(2,128)}, u32[]{:S(2)}) copy-start(s32[2,4,2,128]{3,2,1,0:T(2,128)} %param.10) | copy-start | bytes 24580
  0.6 8.6 %copy-start.2 = (bf16[2,4,128,1024]{3,2,1,0:T(8,128)(2,1)S(1)}, bf16[2,4,128,1024]{3,2,1,0:T(8,128)(2,1)}, u32[]{:S(2)}) copy-start(bf16[2,4,128,1024]{3,2,1,0:T(8,128)(2,1)} %param.8) | copy-start | bytes 6291460
  0.6 8.6 %copy-start.3 = (f32[2,4,128]{2,1,0:T(4,128)S(1)}, f32[2,4,128]{2,1,0:T(4,128)}, u32[]{:S(2)}) copy-start(f32[2,4,128]{2,1,0:T(4,128)} %param.9) | copy-start | bytes 12292
  12.2 3.9 collective-permute-start
  14.6 8.5 %copy-start.1 = (s32[1,1,40,3]{2,1,3,0:T(1,128)S(1)}, s32[1,1,40,3]{2,1,3,0:T(1,128)}, u32[]{:S(2)}) copy-start(s32[1,1,40,3]{2,1,3,0:T(1,128)} %param.11) | copy-start | bytes 1444
  14.6 5.9 %collective-permute-start.1 = (bf16[2,1,128,1024]{3,2,1,0:T(8,128)(2,1)S(1)}, bf16[2,1,128,1024]{3,2,1,0:T(8,128)(2,1)S(1)}, u32[]{:S(2)}, u32[]{:S(2)}) collective-permute-start(bf16[2,1,128,1024]{3,2,1,0:T(8,128)(2,1)S(1)} %get-tuple-element.122), channel_id=1, source_target_pairs={{1,0},{2,1},{3,2},{4,3},{5,4},{6,5},{7,6},{9,8},{10,9},{11,10},{12... | collective-permute-start | bytes 1572872 | tf_op jit(solution)/shard_map/ppermute | solution.py:18
  21.8 30.0 %collective-permute-start.2 = (bf16[1,6,128,1024]{3,2,1,0:T(8,128)(2,1)}, bf16[1,6,128,1024]{3,2,1,0:T(8,128)(2,1)}, u32[]{:S(2)}, u32[]{:S(2)}) collective-permute-start(bf16[1,6,128,1024]{3,2,1,0:T(8,128)(2,1)} %pad_maximum_fusion.1), channel_id=1, source_target_pairs={{8,0},{16,8},{24,16},{9,1},{17,9},{25,17},{10,2},{18,10},{26,18},{... | collective-permute-start | bytes 4718600 | tf_op jit(solution)/shard_map/ppermute | solution.py:26
where the time goes:
time: 464 us; the launch traced here: 457 us
  loops' own time  174 us (38%)
  matrix products  66.7 us (14%)
  other arithmetic  62.7 us (14%)
  local copies, waits for them, and re-layouts  57.8 us (12%)
  blocking collectives  56.5 us (12%)
  waiting for transfers between devices  33.2 us (7%)
  starting transfers between devices  5 us (1%)
    another operation x1, loops' own time, per_device(): sums, counts = lax.fori_loop(0, live_count, add_live, start_value)  174 us
    dot_general x38, matrix products, block_term(): jnp.dot(onehot.reshape(n_sep * per_cell, per_cell), right, preferred_elem...  63.4 us
    psum x1, blocking collectives, per_device(): summed, all_counts = lax.psum((binned, counts), ('ra', 'dec'))  56.5 us
    mul x38, other arithmetic, block_term(): block_sum = jnp.sum(mixed * left.astype(jnp.float32)[None], axis=1)  37.8 us
    eq x38, local copies, waits for them, and re-layouts, block_term(): sep_bins[None, :, :] == jnp.arange(n_sep, dtype=jnp.int32)[:, None, None]  32.5 us
    ppermute x1, waiting for transfers between devices, from_behind(): lax.ppermute(value, axis, [(source, source + steps) for source in range(l...  28.7 us
    slice x38, local copies, waits for them, and re-layouts, slot_term(): index_b = (row_a + entry_row[1]) * cols_pad + col_a + entry_row[2]  22.3 us
    reduce_sum x38, other arithmetic, block_term(): pair_counts = jnp.sum(onehot.reshape(n_sep, -1).astype(jnp.float32), axis=1)  9.44 us
  transfers between devices with their start and end apart: 3, of which 3 were waited for; matrix products, arithmetic and copies ran while one was open for 0% of the time, Pallas kernels for 0%

commit v1 on v0

--- a/solution.py
+++ b/solution.py
@@ -5,6 +5,12 @@
 
 NSEP = 8
 NKB = 128
+
+
+def _fit_islands(slab_in):
+    for b in ("dec", "ra"):
+        slab_in = lax.psum(slab_in, b)
+    return slab_in
 
 
 def extended(block, sides, width):
@@ -105,7 +111,7 @@
     sums, counts = lax.fori_loop(0, live_count, add_live, start_value)
     binned = jnp.dot(sums, kbin_table(length // 2, NKB), precision=lax.Precision.HIGHEST)
     tile_power = (binned / (per_cell * length)).reshape(1, 1, NSEP, NKB)
-    summed, all_counts = lax.psum((binned, counts), ("ra", "dec"))
+    summed, all_counts = _fit_islands((binned, counts))
     sky_power = summed / jnp.maximum(all_counts, 1.0)[:, None]
     return (tile_power, sky_power)
 

time: 464 us -> 446 us (0.961)
  blocking collectives: 56.5 us -> 40.7 us
    psum x1 -> x2, blocking collectives: 56.5 us -> 40.7 us  [_fit_islands(): slab_in = lax.psum(slab_in, b)]
where the time goes in v1:
time: 446 us; the launch traced here: 439 us
  loops' own time  172 us (39%)
  matrix products  66.6 us (15%)
  other arithmetic  62.7 us (14%)
  local copies, waits for them, and re-layouts  57.1 us (13%)
  blocking collectives  40.7 us (9%)
  waiting for transfers between devices  33.2 us (7%)
  starting transfers between devices  5 us (1%)
    another operation x1, loops' own time, per_device(): sums, counts = lax.fori_loop(0, live_count, add_live, start_value)  172 us
    dot_general x38, matrix products, block_term(): jnp.dot(onehot.reshape(n_sep * per_cell, per_cell), right, preferred_elem...  63.4 us
    psum x2, blocking collectives, _fit_islands(): slab_in = lax.psum(slab_in, b)  40.7 us
    mul x38, other arithmetic, block_term(): block_sum = jnp.sum(mixed * left.astype(jnp.float32)[None], axis=1)  37.8 us
    eq x38, local copies, waits for them, and re-layouts, block_term(): sep_bins[None, :, :] == jnp.arange(n_sep, dtype=jnp.int32)[:, None, None]  32.5 us
    ppermute x1, waiting for transfers between devices, from_behind(): lax.ppermute(value, axis, [(source, source + steps) for source in range(l...  28.7 us
    slice x38, local copies, waits for them, and re-layouts, slot_term(): index_b = (row_a + entry_row[1]) * cols_pad + col_a + entry_row[2]  21.6 us
    reduce_sum x38, other arithmetic, block_term(): pair_counts = jnp.sum(onehot.reshape(n_sep, -1).astype(jnp.float32), axis=1)  9.44 us
  transfers between devices with their start and end apart: 3, of which 3 were waited for; matrix products, arithmetic and copies ran while one was open for 0% of the time, Pallas kernels for 0%

profile of v1, /device:TPU:0, one launch (start us, length us, event | category | flops | bytes accessed | tf_op | source)
XLA Modules:
  0.0 438.7 jit_solution(1928310419859316378)
XLA Ops:
  0.7 8.5 %sine_convert_fusion = (bf16[1024,512]{1,0:T(8,128)(2,1)S(1)}, bf16[1024,512]{1,0:T(8,128)(2,1)S(1)}) fusion(), kind=kLoop, calls=%fused_computation.29 | loop fusion | flops 8388608 | bytes 2097152 | tf_op jit(solution)/shard_map/convert.2
  9.2 2.9 multiply_convert_fusion
  12.2 2.4 collective-permute-start
  16.1 4.4 %collective-permute-done.1 = bf16[2,1,128,1024]{3,2,1,0:T(8,128)(2,1)S(1)} collective-permute-done((bf16[2,1,128,1024]{3,2,1,0:T(8,128)(2,1)S(1)}, bf16[2,1,128,1024]{3,2,1,0:T(8,128)(2,1)S(1)}, u32[]{:S(2)}, u32[]{:S(2)}) %collective-permute-start.1) | collective-permute-done | bytes 524320 | tf_op jit(solution)/shard_map/ppermute | solution.py:24
  23.2 28.7 %collective-permute-done.2 = bf16[1,6,128,1024]{3,2,1,0:T(8,128)(2,1)} collective-permute-done((bf16[1,6,128,1024]{3,2,1,0:T(8,128)(2,1)}, bf16[1,6,128,1024]{3,2,1,0:T(8,128)(2,1)}, u32[]{:S(2)}, u32[]{:S(2)}) %collective-permute-start.2) | collective-permute-done | bytes 1572896 | tf_op jit(solution)/shard_map/ppermute | solution.py:32
  51.8 3.6 pad_maximum_fusion
  55.4 340.8 %while.14 = (s32[]{:T(128)}, f32[8,1024]{1,0:T(8,128)S(1)}, f32[8]{0:T(128)S(1)}, s32[]{:T(128)}, s32[40,128,128]{2,1,0:T(8,128)}, /*index=5*/s32[40,3]{0,1:T(4,...) while((s32[]{:T(128)}, f32[8,1024]{1,0:T(8,128)S(1)}, ...), condition=%wide.region_3.4_spmd, body=%wide.region_0.3_spmd.sunk | while | flops 271319072 | bytes 2032330 | solution.py:111
  62.4 1.7 multiply_reduce_fusion.2
  71.4 1.7 multiply_reduce_fusion.2
  80.3 1.7 multiply_reduce_fusion.2
  89.3 1.7 multiply_reduce_fusion.2
  98.2 1.7 multiply_reduce_fusion.2
  107.2 1.7 multiply_reduce_fusion.2
  116.1 1.7 multiply_reduce_fusion.2
  125.1 1.7 multiply_reduce_fusion.2
  134.0 1.7 multiply_reduce_fusion.2
  143.0 1.7 multiply_reduce_fusion.2
  151.9 1.7 multiply_reduce_fusion.2
  160.9 1.7 multiply_reduce_fusion.2
  169.8 1.7 multiply_reduce_fusion.2
  178.8 1.7 multiply_reduce_fusion.2
  187.7 1.7 multiply_reduce_fusion.2
  196.7 1.7 multiply_reduce_fusion.2
  205.6 1.7 multiply_reduce_fusion.2
  214.6 1.7 multiply_reduce_fusion.2
  223.5 1.7 multiply_reduce_fusion.2
  232.5 1.7 multiply_reduce_fusion.2
  241.4 1.7 multiply_reduce_fusion.2
  250.4 1.7 multiply_reduce_fusion.2
  259.4 1.7 multiply_reduce_fusion.2
  397.2 12.1 %all-reduce = (f32[8,128]{1,0:T(8,128)S(1)}, f32[8]{0:T(128)S(1)}) all-reduce(f32[8,128]{1,0:T(8,128)S(1)} %fusion.21, f32[8]{0:T(128)S(1)} %get-tuple-element.99), channel_id=1, replica_groups=mesh['ra'=4,'dec'=8] {'dec'}, use_global_device_ids=true, to_apply=%region_4.5 | all-reduce | flops 1032 | bytes 8256 | tf_op jit(solution)/shard_map/psum | solution.py:12
  409.3 28.6 %all-reduce.1 = (f32[8,128]{1,0:T(8,128)S(1)}, f32[8]{0:T(128)S(1)}) all-reduce(f32[8,128]{1,0:T(8,128)S(1)} %get-tuple-element.114, f32[8]{0:T(128)S(1)} %get-tuple-element.115), channel_id=1, replica_groups=mesh['ra'=4,'dec'=8] {'ra'}, use_global_device_ids=true, to_apply=%region_5.6 | all-reduce | flops 1032 | bytes 8256 | tf_op jit(solution)/shard_map/psum | solution.py:12
  (305 shorter events, 135.9 us)
Async XLA Ops:
  0.6 8.5 %copy-start = (s32[2,4,2,128]{3,2,1,0:T(2,128)S(1)}, s32[2,4,2,128]{3,2,1,0:T(2,128)}, u32[]{:S(2)}) copy-start(s32[2,4,2,128]{3,2,1,0:T(2,128)} %param.10) | copy-start | bytes 24580
  0.6 8.6 %copy-start.2 = (bf16[2,4,128,1024]{3,2,1,0:T(8,128)(2,1)S(1)}, bf16[2,4,128,1024]{3,2,1,0:T(8,128)(2,1)}, u32[]{:S(2)}) copy-start(bf16[2,4,128,1024]{3,2,1,0:T(8,128)(2,1)} %param.8) | copy-start | bytes 6291460
  0.6 8.6 %copy-start.3 = (f32[2,4,128]{2,1,0:T(4,128)S(1)}, f32[2,4,128]{2,1,0:T(4,128)}, u32[]{:S(2)}) copy-start(f32[2,4,128]{2,1,0:T(4,128)} %param.9) | copy-start | bytes 12292
  12.2 3.9 collective-permute-start
  14.6 8.5 %copy-start.1 = (s32[1,1,40,3]{2,1,3,0:T(1,128)S(1)}, s32[1,1,40,3]{2,1,3,0:T(1,128)}, u32[]{:S(2)}) copy-start(s32[1,1,40,3]{2,1,3,0:T(1,128)} %param.11) | copy-start | bytes 1444
  14.6 5.9 %collective-permute-start.1 = (bf16[2,1,128,1024]{3,2,1,0:T(8,128)(2,1)S(1)}, bf16[2,1,128,1024]{3,2,1,0:T(8,128)(2,1)S(1)}, u32[]{:S(2)}, u32[]{:S(2)}) collective-permute-start(bf16[2,1,128,1024]{3,2,1,0:T(8,128)(2,1)S(1)} %get-tuple-element.124), channel_id=1, source_target_pairs={{1,0},{2,1},{3,2},{4,3},{5,4},{6,5},{7,6},{9,8},{10,9},{11,10},{12... | collective-permute-start | bytes 1572872 | tf_op jit(solution)/shard_map/ppermute | solution.py:24
  21.9 30.0 %collective-permute-start.2 = (bf16[1,6,128,1024]{3,2,1,0:T(8,128)(2,1)}, bf16[1,6,128,1024]{3,2,1,0:T(8,128)(2,1)}, u32[]{:S(2)}, u32[]{:S(2)}) collective-permute-start(bf16[1,6,128,1024]{3,2,1,0:T(8,128)(2,1)} %pad_maximum_fusion.1), channel_id=1, source_target_pairs={{8,0},{16,8},{24,16},{9,1},{17,9},{25,17},{10,2},{18,10},{26,18},{... | collective-permute-start | bytes 4718600 | tf_op jit(solution)/shard_map/ppermute | solution.py:32
